TPU v7x, 128 devices: a whole 4x4x4 slice. The times are simulated.
128 devices in a mesh: dp: 8 (over x, core), fsdp: 16 (over z, y).
Axes of the slice: x: 4, y: 4, z: 4, core: 2. Of those that a mesh axis runs over, the one named last changes fastest.
Arguments:
- tokens: bfloat16 [65536, 1408], P(('dp', 'fsdp')), may hold values from -6 to 6
- image_of: int32 [65536], P(('dp', 'fsdp')), may hold values from 0 to 16383, as said below
- live: int32 [65536], P(('dp', 'fsdp')), may hold values from 0 to 1, as said below
- request_of: int32 [16384], P('dp'), may hold values from -1 to 63, as said below
- ln1_gain: float32 [1408], replicated, may hold values from 0.5 to 1.5
- ln1_shift: float32 [1408], replicated, may hold values from -3 to 3
- w_qkv: bfloat16 [1408, 4224], P('fsdp')
- b_qkv: float32 [4224], replicated, may hold values from -3 to 3
- w_out: bfloat16 [1408, 1408], P('fsdp'), may hold values from -0.15625 to 0.15625
- b_out: float32 [1408], replicated, may hold values from -3 to 3
- ln2_gain: float32 [1408], replicated, may hold values from 0.5 to 1.5
- ln2_shift: float32 [1408], replicated, may hold values from -3 to 3
- w_proj: bfloat16 [5632, 4096], P(None, 'fsdp'), may hold values from -0.078125 to 0.078125
- b_proj: float32 [4096], P('fsdp'), may hold values from -3 to 3
Outputs:
- features: bfloat16 [16384, 4096], P('dp', 'fsdp')
- peaks: float32 [64], replicated
Inputs may be any that keep to these rules, and one draw needn't show every extreme that they name: `image_of`: tokens come in aligned groups of 4 of one image; an image's tokens are consecutive and lie within one aligned block of 512 rows; numbers never fall along the rows; the last block's last group of 4 is an image of its own. Padding fills whole groups of 4 at the end of each aligned block of 512 rows, at most half of the block; the first group of every block is live and the last block has none; a padding token carries the image number of the token before it. `request_of`: -1 exactly on merged rows of padding; on the other rows request numbers never fall along the rows, and every request has some row.
All inputs are finite; a program needn't handle non-finite values.
Results may differ from a plain program's by a relative error of at most 0.012.
The roundings to bfloat16 on the way count: a program that leaves them out, or rounds other values in their place, can miss the bound.
Values may be sent and summed in bfloat16 or wider, within the bound.
A program may use at most 192 MiB of HBM per device.

v0:
```python
import jax
import jax.numpy as jnp
from jax import lax
from jax.sharding import PartitionSpec as P

HEADS = 16


def normalize(values, gain, shift):
    mean_value = jnp.mean(values, axis=-1, keepdims=True)
    centred = values - mean_value
    variance = jnp.mean(centred * centred, axis=-1, keepdims=True)
    return centred * lax.rsqrt(variance + 1e-06) * gain + shift


def attention(qkv, image_ids, live_flags, heads):
    count_rows = qkv.shape[0]
    width = qkv.shape[1] // 3
    head_size = width // heads
    scale = head_size ** (-0.5)
    queries = qkv[:, :width].reshape(count_rows, heads, head_size)
    keys_all = qkv[:, width : 2 * width].reshape(count_rows, heads, head_size)
    values_all = qkv[:, 2 * width :].reshape(count_rows, heads, head_size)
    block_rows = min(512, count_rows)
    blocks = count_rows // block_rows
    key_live = live_flags[None, :] == 1

    def one_block(items):
        block_queries, block_images = items
        scores = (
            jnp.einsum("qhe,khe->hqk", block_queries, keys_all, preferred_element_type=jnp.float32)
            * scale
        )
        allowed = (block_images[:, None] == image_ids[None, :]) & key_live
        scores = jnp.where(allowed[None], scores, jnp.float32(-1e30))
        top = jnp.max(scores, axis=-1, keepdims=True)
        expo = jnp.exp(scores - top)
        weights = (expo / jnp.sum(expo, axis=-1, keepdims=True)).astype(jnp.bfloat16)
        mixed = jnp.einsum("hqk,khe->qhe", weights, values_all, preferred_element_type=jnp.float32)
        return mixed.reshape(block_rows, width).astype(jnp.bfloat16)

    result = lax.map(
        one_block,
        (
            queries.reshape(blocks, block_rows, heads, head_size),
            image_ids.reshape(blocks, block_rows),
        ),
    )
    return result.reshape(count_rows, width)


def shards(
    tokens,
    image_of,
    live,
    request_of,
    ln1_gain,
    ln1_shift,
    w_qkv,
    b_qkv,
    w_out,
    b_out,
    ln2_gain,
    ln2_shift,
    w_proj,
    b_proj,
):
    count_rows = tokens.shape[0]
    width = tokens.shape[1]
    resid = tokens.astype(jnp.float32)
    normed = normalize(resid, ln1_gain, ln1_shift).astype(jnp.bfloat16)
    columns = normed
    mixed = jnp.dot(
        columns,
        lax.all_gather(w_qkv, "fsdp", axis=0, tiled=True),
        preferred_element_type=jnp.float32,
    )
    qkv = (mixed + b_qkv).astype(jnp.bfloat16)
    attended = attention(qkv, image_of, live, HEADS)
    columns = attended
    projected_out = jnp.dot(
        columns,
        lax.all_gather(w_out, "fsdp", axis=0, tiled=True),
        preferred_element_type=jnp.float32,
    )
    resid = resid + (projected_out + b_out)
    normed2 = normalize(resid, ln2_gain, ln2_shift).astype(jnp.bfloat16)
    merged = normed2.reshape(count_rows // 4, 4 * width)
    projected = (
        jnp.dot(
            lax.all_gather(merged, "fsdp", axis=0, tiled=True),
            w_proj,
            preferred_element_type=jnp.float32,
        )
        + b_proj
    )
    requests = lax.axis_size("dp") * lax.axis_size("fsdp") // 2
    columns_here = projected.shape[1]
    labels = jnp.arange(requests, dtype=jnp.int32)
    member = request_of[:, None] == labels[None, :]
    row_squares = jnp.sum(projected * projected, axis=1)
    row_top = jnp.max(projected, axis=1)
    sums_part = jnp.sum(jnp.where(member, row_squares[:, None], jnp.float32(0.0)), axis=0)
    entries_part = jnp.sum(member.astype(jnp.float32), axis=0) * jnp.float32(columns_here)
    top_part = jnp.max(jnp.where(member, row_top[:, None], jnp.float32(-jnp.inf)), axis=0)
    sumsq, entries = lax.psum((sums_part, entries_part), ("dp", "fsdp"))
    top = lax.pmax(top_part, ("dp", "fsdp"))
    rms = jnp.sqrt(sumsq / entries + 1e-06)
    valid = request_of >= 0
    row_rms = jnp.sum(jnp.where(member, rms[None, :], jnp.float32(0.0)), axis=1) + jnp.where(
        valid, 0.0, 1.0
    )
    features = jnp.where(valid[:, None], projected / row_rms[:, None], jnp.float32(0.0)).astype(
        jnp.bfloat16
    )
    peaks = top / rms
    return (features, peaks)


def solution(mesh):
    return jax.shard_map(
        shards,
        mesh=mesh,
        in_specs=(
            P(("dp", "fsdp"), None),
            P(("dp", "fsdp")),
            P(("dp", "fsdp")),
            P("dp"),
            P(),
            P(),
            P("fsdp", None),
            P(),
            P("fsdp", None),
            P(),
            P(),
            P(),
            P(None, "fsdp"),
            P("fsdp"),
        ),
        out_specs=(P("dp", "fsdp"), P()),
        check_vma=False,
    )
```

profile of v0, /device:TPU:1, one launch (start us, length us, event | category | flops | bytes accessed | tf_op | source)
XLA Modules:
  0.0 461.9 jit_solution(2938531197813447947)
XLA Ops:
  7.3 0.7 all-gather.4.cloned.1.call-update
  8.0 0.7 all-gather.6.cloned.1.call-update
  8.8 1.6 convert_reduce_fusion
  10.4 1.9 fusion.8
  12.6 87.9 %all-gather.4.cloned.1.call-done = bf16[1408,4224]{1,0:T(8,128)(2,1)} async-done(((bf16[88,4224]{1,0:T(8,128)(2,1)}), bf16[1408,4224]{1,0:T(8,128)(2,1)}) %all-gather.4.cloned.1.call-update) | async-done | bytes 11894800 | tf_op jit(solution)/shard_map/all_gather | solution.py:75
  100.5 12.4 %add_convert_fusion = bf16[512,4224]{1,0:T(8,128)(2,1)S(1)} fusion(bf16[1408,4224]{1,0:T(8,128)(2,1)} %all-gather.4.cloned.1.call-done, f32[4224]{0:T(1024)S(1)} %copy-done.7, bf16[512,1408]{1,0:T(8,128)(2,1)} %param.14, f32[1408]{0:T(1024)S(1)} %copy-done.8, f32[1408]{0:T(1024)S(1)} %copy-done.9, f32[512]{0:T(512)S(1)} %add_rsqrt_fusion.1, ...), kind=kOutput, calls=%fused_computation.5 | convolution fusion | flops 6098780160 | bytes 17694208 | tf_op jit(solution)/shard_map/dot_general | solution.py:73
  112.8 2.1 fusion.23
  115.0 2.6 copy.27
  117.6 2.5 copy.28
  120.1 2.6 copy.26
  122.7 11.0 %fusion.24 = (f32[16,512]{1,0:T(8,128)S(1)}, f32[16,512,512]{1,2,0:T(8,128)}) fusion(pred[512,512]{0,1:T(8,128)(4,1)S(1)} %compare_and_fusion, bf16[512,16,88]{0,2,1:T(8,128)(2,1)} %bitcast.17, bf16[512,16,88]{0,2,1:T(8,128)(2,1)} %bitcast.18), kind=kOutput, calls=%fused_computation.50 | convolution fusion | flops 754975232 | bytes 19955712 | tf_op jit(solution)/shard_map/while/body/eval_jaxpr/sub | solution.py:37
  133.7 8.9 %fusion.14 = bf16[16,88,512]{2,1,0:T(8,128)(2,1)} fusion(bf16[512,16,88]{0,2,1:T(8,128)(2,1)} %bitcast.19, f32[16,512,512]{1,2,0:T(8,128)} %get-tuple-element.46, f32[16,512]{1,0:T(8,128)S(1)} %get-tuple-element.45), kind=kOutput, calls=%fused_computation.26 | convolution fusion | flops 747307008 | bytes 19693568 | tf_op jit(solution)/shard_map/while/body/eval_jaxpr/hqk,khe->qhe/dot_general | solution.py:39
  142.5 10.3 %all-gather.6.cloned.1.call-done = bf16[1408,1408]{1,0:T(8,128)(2,1)} async-done(((bf16[88,1408]{1,0:T(8,128)(2,1)}), bf16[1408,1408]{1,0:T(8,128)(2,1)}) %all-gather.6.cloned.1.call-update) | async-done | bytes 3964944 | tf_op jit(solution)/shard_map/all_gather | solution.py:83
  152.9 5.9 %fusion.25 = (f32[512]{0:T(512)S(1)}, f32[512,1408]{1,0:T(8,128)S(1)}) fusion(f32[1408]{0:T(1024)S(1)} %copy-done.2, bf16[512,1408]{0,1:T(8,128)(2,1)} %bitcast.16, bf16[1408,1408]{1,0:T(8,128)(2,1)} %all-gather.6.cloned.1.call-done, bf16[512,1408]{1,0:T(8,128)(2,1)} %param.14), kind=kOutput, calls=%fused_computation.51 | convolution fusion | flops 2032926208 | bytes 9739776 | tf_op jit(solution)/shard_map/dot_general | solution.py:81
  158.8 0.4 multiply_reduce_fusion
  159.5 1.7 add_convert_fusion.1
  161.2 3.6 reshape.109
  164.8 143.3 %all-gather.8.cloned.1.call-done = bf16[2048,5632]{1,0:T(8,128)(2,1)} async-done(((bf16[128,5632]{1,0:T(8,128)(2,1)}), bf16[2048,5632]{1,0:T(8,128)(2,1)}) %all-gather.8.cloned.1.call-update) | async-done | bytes 23068688 | tf_op jit(solution)/shard_map/all_gather | solution.py:91
  308.2 12.5 %fusion.22 = (f32[2048]{0:T(1024)S(1)}, f32[2048]{0:T(1024)S(1)}, f32[2048,256]{0,1:T(8,128)}) fusion(f32[256]{0:T(256)S(1)} %copy-done.10, bf16[2048,5632]{1,0:T(8,128)(2,1)} %all-gather.8.cloned.1.call-done, bf16[5632,256]{1,0:T(8,128)(2,1)S(1)} %copy-done), kind=kOutput, calls=%fused_computation.48 | convolution fusion | flops 5907673088 | bytes 28066816 | tf_op jit(solution)/shard_map/dot_general | solution.py:90
  320.9 64.6 %all-reduce = (f32[64]{0:T(128)S(1)}, f32[64]{0:T(128)S(1)}) all-reduce(f32[64]{0:T(128)S(1)} %get-tuple-element.37, f32[64]{0:T(128)S(1)} %broadcast_multiply_fusion.2), channel_id=1, replica_groups=mesh['dp'=8,'fsdp'=16] {'dp','fsdp'}, use_global_device_ids=true, to_apply=%region_8.9 | all-reduce | flops 128 | bytes 1024 | tf_op jit(solution)/shard_map/psum | solution.py:106
  385.7 64.1 %pmax.7 = f32[64]{0:T(128)S(1)} all-reduce(f32[64]{0:T(128)S(1)} %get-tuple-element.34), channel_id=1, replica_groups=mesh['dp'=8,'fsdp'=16] {'dp','fsdp'}, use_global_device_ids=true, to_apply=%region_14.15 | all-reduce | flops 64 | bytes 512 | tf_op jit(solution)/shard_map/pmax | solution.py:107
  449.8 0.5 div.47
  450.3 2.8 select_convert_fusion
  453.2 2.3 copy.30
  (37 shorter events, 1.1 us)
Async XLA Ops:
  7.2 301.0 %copy-start = (bf16[5632,256]{1,0:T(8,128)(2,1)S(1)}, bf16[5632,256]{1,0:T(8,128)(2,1)}, u32[]{:S(2)}) copy-start(bf16[5632,256]{1,0:T(8,128)(2,1)} %param.26) | copy-start | bytes 8650756
  7.2 5.1 %copy-start.6 = (s32[512]{0:T(512)S(1)}, s32[512]{0:T(512)}, u32[]{:S(2)}) copy-start(s32[512]{0:T(512)} %param.16) | copy-start | bytes 6148
  7.2 5.1 %copy-start.5 = (s32[512]{0:T(512)S(1)}, s32[512]{0:T(512)}, u32[]{:S(2)}) copy-start(s32[512]{0:T(512)} %param.15) | copy-start | bytes 6148
  7.2 93.3 %copy-start.9 = (f32[1408]{0:T(1024)S(1)}, f32[1408]{0:T(1024)}, u32[]{:S(2)}) copy-start(f32[1408]{0:T(1024)} %param.18) | copy-start | bytes 16900
  7.2 93.3 %copy-start.8 = (f32[1408]{0:T(1024)S(1)}, f32[1408]{0:T(1024)}, u32[]{:S(2)}) copy-start(f32[1408]{0:T(1024)} %param.19) | copy-start | bytes 16900
  7.2 93.3 %copy-start.7 = (f32[4224]{0:T(1024)S(1)}, f32[4224]{0:T(1024)}, u32[]{:S(2)}) copy-start(f32[4224]{0:T(1024)} %param.21) | copy-start | bytes 50692
  7.2 93.2 %all-gather.4.cloned.1.call-start = ((), (), s32[]{:S(2)}) async-start(), calls=%async_computation | async-start | bytes 12638208 | tf_op jit(solution)/shard_map/all_gather | solution.py:75
  8.0 144.9 %all-gather.6.cloned.1.call-start = ((), (), s32[]{:S(2)}) async-start(), calls=%async_computation.1 | async-start | bytes 4212736 | tf_op jit(solution)/shard_map/all_gather | solution.py:83
  8.7 299.4 %all-gather.8.cloned.1.call-start = ((), (), s32[]{:S(2)}) async-start(), calls=%async_computation.2 | async-start | bytes 24510464 | tf_op jit(solution)/shard_map/all_gather | solution.py:91
  133.7 19.2 %copy-start.2 = (f32[1408]{0:T(1024)S(1)}, f32[1408]{0:T(1024)}, u32[]{:S(2)}) copy-start(f32[1408]{0:T(1024)} %param.23) | copy-start | bytes 16900
  158.8 0.7 copy-start.3
  158.8 0.7 copy-start.4
  161.2 147.0 %copy-start.10 = (f32[256]{0:T(256)S(1)}, f32[256]{0:T(256)}, u32[]{:S(2)}) copy-start(f32[256]{0:T(256)} %param.27) | copy-start | bytes 3076
  164.8 155.8 %copy-start.1 = (s32[2048]{0:T(1024)S(1)}, s32[2048]{0:T(1024)}, u32[]{:S(2)}) copy-start(s32[2048]{0:T(1024)} %param.17) | copy-start | bytes 24580
Sparse Core Ops, SparseCore 0:
  10.2 90.2 all-gather.3
  102.6 50.2 all-gather.5
  164.9 143.1 all-gather.7
where the time goes:
time: 462 us
  waiting for transfers between devices  243 us (53%)
  blocking collectives  129 us (28%)
  matrix products  50.6 us (11%)
  local copies, waits for them, and re-layouts  16 us (3%)
  between operations  13.9 us (3%)
  other arithmetic  9.62 us (2%)
    all_gather x1, waiting for transfers between devices, shards(): lax.all_gather(merged, 'fsdp', axis=0, tiled=True)  143 us
    all_gather x1, waiting for transfers between devices, shards(): lax.all_gather(w_qkv, 'fsdp', axis=0, tiled=True)  87.9 us
    psum x1, blocking collectives, shards(): sumsq, entries = lax.psum((sums_part, entries_part), ('dp', 'fsdp'))  64.6 us
    pmax x1, blocking collectives, shards(): top = lax.pmax(top_part, ('dp', 'fsdp'))  64.1 us
    dot_general x1, matrix products, shards(): jnp.dot(lax.all_gather(merged, 'fsdp', axis=0, tiled=True), w_proj, prefe...  12.5 us
    dot_general x1, matrix products, shards(): jnp.dot(columns, lax.all_gather(w_qkv, 'fsdp', axis=0, tiled=True), prefe...  12.4 us
    sub x1, matrix products, one_block(): expo = jnp.exp(scores - top)  11 us
    all_gather x1, waiting for transfers between devices, shards(): lax.all_gather(w_out, 'fsdp', axis=0, tiled=True)  10.3 us
  transfers between devices with their start and end apart: 3, of which 3 were waited for; matrix products, arithmetic and copies ran while one was open for 10% of the time, Pallas kernels for 0%

commit v1 on v0

--- a/solution.py
+++ b/solution.py
@@ -103,7 +103,7 @@
     sums_part = jnp.sum(jnp.where(member, row_squares[:, None], jnp.float32(0.0)), axis=0)
     entries_part = jnp.sum(member.astype(jnp.float32), axis=0) * jnp.float32(columns_here)
     top_part = jnp.max(jnp.where(member, row_top[:, None], jnp.float32(-jnp.inf)), axis=0)
-    sumsq, entries = lax.psum((sums_part, entries_part), ("dp", "fsdp"))
+    sumsq, entries = lax.psum(lax.psum((sums_part, entries_part), "fsdp"), "dp")
     top = lax.pmax(top_part, ("dp", "fsdp"))
     rms = jnp.sqrt(sumsq / entries + 1e-06)
     valid = request_of >= 0

time: 462 us -> 447 us (0.968)
  blocking collectives: 129 us -> 113 us
    psum x1 -> x2, blocking collectives: 64.6 us -> 50.9 us  [shards(): sumsq, entries = lax.psum(lax.psum((sums_part, entries_part), 'fsdp'), 'dp')]
where the time goes in v1:
time: 447 us; the launch traced here: 446 us
  waiting for transfers between devices  243 us (54%)
  blocking collectives  113 us (25%)
  matrix products  50.6 us (11%)
  local copies, waits for them, and re-layouts  16 us (4%)
  between operations  13.9 us (3%)
  other arithmetic  9.62 us (2%)
    all_gather x1, waiting for transfers between devices, shards(): lax.all_gather(merged, 'fsdp', axis=0, tiled=True)  143 us
    all_gather x1, waiting for transfers between devices, shards(): lax.all_gather(w_qkv, 'fsdp', axis=0, tiled=True)  87.9 us
    pmax x1, blocking collectives, shards(): top = lax.pmax(top_part, ('dp', 'fsdp'))  62 us
    psum x2, blocking collectives, shards(): sumsq, entries = lax.psum(lax.psum((sums_part, entries_part), 'fsdp'), 'dp')  50.9 us
    dot_general x1, matrix products, shards(): jnp.dot(lax.all_gather(merged, 'fsdp', axis=0, tiled=True), w_proj, prefe...  12.5 us
    dot_general x1, matrix products, shards(): jnp.dot(columns, lax.all_gather(w_qkv, 'fsdp', axis=0, tiled=True), prefe...  12.4 us
    sub x1, matrix products, one_block(): expo = jnp.exp(scores - top)  11 us
    all_gather x1, waiting for transfers between devices, shards(): lax.all_gather(w_out, 'fsdp', axis=0, tiled=True)  10.3 us
  transfers between devices with their start and end apart: 3, of which 3 were waited for; matrix products, arithmetic and copies ran while one was open for 10% of the time, Pallas kernels for 0%

profile of v1, /device:TPU:1, one launch (start us, length us, event | category | flops | bytes accessed | tf_op | source)
XLA Modules:
  0.0 446.2 jit_solution(5782734841469964721)
XLA Ops:
  7.3 0.7 all-gather.4.cloned.1.call-update
  8.0 0.7 all-gather.6.cloned.1.call-update
  8.8 1.6 convert_reduce_fusion
  10.4 1.9 fusion.8
  12.6 87.9 %all-gather.4.cloned.1.call-done = bf16[1408,4224]{1,0:T(8,128)(2,1)} async-done(((bf16[88,4224]{1,0:T(8,128)(2,1)}), bf16[1408,4224]{1,0:T(8,128)(2,1)}) %all-gather.4.cloned.1.call-update) | async-done | bytes 11894800 | tf_op jit(solution)/shard_map/all_gather | solution.py:75
  100.5 12.4 %add_convert_fusion = bf16[512,4224]{1,0:T(8,128)(2,1)S(1)} fusion(bf16[1408,4224]{1,0:T(8,128)(2,1)} %all-gather.4.cloned.1.call-done, f32[4224]{0:T(1024)S(1)} %copy-done.7, bf16[512,1408]{1,0:T(8,128)(2,1)} %param.14, f32[1408]{0:T(1024)S(1)} %copy-done.8, f32[1408]{0:T(1024)S(1)} %copy-done.9, f32[512]{0:T(512)S(1)} %add_rsqrt_fusion.1, ...), kind=kOutput, calls=%fused_computation.5 | convolution fusion | flops 6098780160 | bytes 17694208 | tf_op jit(solution)/shard_map/dot_general | solution.py:73
  112.8 2.1 fusion.23
  115.0 2.6 copy.27
  117.6 2.5 copy.28
  120.1 2.6 copy.26
  122.7 11.0 %fusion.24 = (f32[16,512]{1,0:T(8,128)S(1)}, f32[16,512,512]{1,2,0:T(8,128)}) fusion(pred[512,512]{0,1:T(8,128)(4,1)S(1)} %compare_and_fusion, bf16[512,16,88]{0,2,1:T(8,128)(2,1)} %bitcast.17, bf16[512,16,88]{0,2,1:T(8,128)(2,1)} %bitcast.18), kind=kOutput, calls=%fused_computation.50 | convolution fusion | flops 754975232 | bytes 19955712 | tf_op jit(solution)/shard_map/while/body/eval_jaxpr/sub | solution.py:37
  133.7 8.9 %fusion.14 = bf16[16,88,512]{2,1,0:T(8,128)(2,1)} fusion(bf16[512,16,88]{0,2,1:T(8,128)(2,1)} %bitcast.19, f32[16,512,512]{1,2,0:T(8,128)} %get-tuple-element.48, f32[16,512]{1,0:T(8,128)S(1)} %get-tuple-element.47), kind=kOutput, calls=%fused_computation.26 | convolution fusion | flops 747307008 | bytes 19693568 | tf_op jit(solution)/shard_map/while/body/eval_jaxpr/hqk,khe->qhe/dot_general | solution.py:39
  142.5 10.3 %all-gather.6.cloned.1.call-done = bf16[1408,1408]{1,0:T(8,128)(2,1)} async-done(((bf16[88,1408]{1,0:T(8,128)(2,1)}), bf16[1408,1408]{1,0:T(8,128)(2,1)}) %all-gather.6.cloned.1.call-update) | async-done | bytes 3964944 | tf_op jit(solution)/shard_map/all_gather | solution.py:83
  152.9 5.9 %fusion.25 = (f32[512]{0:T(512)S(1)}, f32[512,1408]{1,0:T(8,128)S(1)}) fusion(f32[1408]{0:T(1024)S(1)} %copy-done.2, bf16[512,1408]{0,1:T(8,128)(2,1)} %bitcast.16, bf16[1408,1408]{1,0:T(8,128)(2,1)} %all-gather.6.cloned.1.call-done, bf16[512,1408]{1,0:T(8,128)(2,1)} %param.14), kind=kOutput, calls=%fused_computation.51 | convolution fusion | flops 2032926208 | bytes 9739776 | tf_op jit(solution)/shard_map/dot_general | solution.py:81
  159.5 1.7 add_convert_fusion.1
  161.2 3.6 reshape.109
  164.8 143.3 %all-gather.8.cloned.1.call-done = bf16[2048,5632]{1,0:T(8,128)(2,1)} async-done(((bf16[128,5632]{1,0:T(8,128)(2,1)}), bf16[2048,5632]{1,0:T(8,128)(2,1)}) %all-gather.8.cloned.1.call-update) | async-done | bytes 23068688 | tf_op jit(solution)/shard_map/all_gather | solution.py:91
  308.2 12.5 %fusion.22 = (f32[2048]{0:T(1024)S(1)}, f32[2048]{0:T(1024)S(1)}, f32[2048,256]{0,1:T(8,128)}) fusion(f32[256]{0:T(256)S(1)} %copy-done.10, bf16[2048,5632]{1,0:T(8,128)(2,1)} %all-gather.8.cloned.1.call-done, bf16[5632,256]{1,0:T(8,128)(2,1)S(1)} %copy-done), kind=kOutput, calls=%fused_computation.48 | convolution fusion | flops 5907673088 | bytes 28066816 | tf_op jit(solution)/shard_map/dot_general | solution.py:90
  320.9 31.6 %all-reduce = (f32[64]{0:T(128)S(1)}, f32[64]{0:T(128)S(1)}) all-reduce(f32[64]{0:T(128)S(1)} %get-tuple-element.37, f32[64]{0:T(128)S(1)} %broadcast_multiply_fusion.2), channel_id=1, replica_groups=mesh['dp'=8,'fsdp'=16] {'fsdp'}, use_global_device_ids=true, to_apply=%region_8.9 | all-reduce | flops 128 | bytes 1024 | tf_op jit(solution)/shard_map/psum | solution.py:106
  352.4 19.4 %all-reduce.1 = (f32[64]{0:T(128)S(1)}, f32[64]{0:T(128)S(1)}) all-reduce(f32[64]{0:T(128)S(1)} %get-tuple-element.38, f32[64]{0:T(128)S(1)} %get-tuple-element.39), channel_id=1, replica_groups=mesh['dp'=8,'fsdp'=16] {'dp'}, use_global_device_ids=true, to_apply=%region_9.10 | all-reduce | flops 128 | bytes 1024 | tf_op jit(solution)/shard_map/psum | solution.py:106
  372.0 62.0 %pmax.7 = f32[64]{0:T(128)S(1)} all-reduce(f32[64]{0:T(128)S(1)} %get-tuple-element.34), channel_id=1, replica_groups=mesh['dp'=8,'fsdp'=16] {'dp','fsdp'}, use_global_device_ids=true, to_apply=%region_16.17 | all-reduce | flops 64 | bytes 512 | tf_op jit(solution)/shard_map/pmax | solution.py:107
  434.0 0.5 div.47
  434.6 2.8 select_convert_fusion
  437.4 2.3 copy.30
  (38 shorter events, 1.5 us)
Async XLA Ops:
  7.2 301.0 %copy-start = (bf16[5632,256]{1,0:T(8,128)(2,1)S(1)}, bf16[5632,256]{1,0:T(8,128)(2,1)}, u32[]{:S(2)}) copy-start(bf16[5632,256]{1,0:T(8,128)(2,1)} %param.26) | copy-start | bytes 8650756
  7.2 5.1 %copy-start.6 = (s32[512]{0:T(512)S(1)}, s32[512]{0:T(512)}, u32[]{:S(2)}) copy-start(s32[512]{0:T(512)} %param.16) | copy-start | bytes 6148
  7.2 5.1 %copy-start.5 = (s32[512]{0:T(512)S(1)}, s32[512]{0:T(512)}, u32[]{:S(2)}) copy-start(s32[512]{0:T(512)} %param.15) | copy-start | bytes 6148
  7.2 93.3 %copy-start.9 = (f32[1408]{0:T(1024)S(1)}, f32[1408]{0:T(1024)}, u32[]{:S(2)}) copy-start(f32[1408]{0:T(1024)} %param.18) | copy-start | bytes 16900
  7.2 93.3 %copy-start.8 = (f32[1408]{0:T(1024)S(1)}, f32[1408]{0:T(1024)}, u32[]{:S(2)}) copy-start(f32[1408]{0:T(1024)} %param.19) | copy-start | bytes 16900
  7.2 93.3 %copy-start.7 = (f32[4224]{0:T(1024)S(1)}, f32[4224]{0:T(1024)}, u32[]{:S(2)}) copy-start(f32[4224]{0:T(1024)} %param.21) | copy-start | bytes 50692
  7.2 93.2 %all-gather.4.cloned.1.call-start = ((), (), s32[]{:S(2)}) async-start(), calls=%async_computation | async-start | bytes 12638208 | tf_op jit(solution)/shard_map/all_gather | solution.py:75
  8.0 144.9 %all-gather.6.cloned.1.call-start = ((), (), s32[]{:S(2)}) async-start(), calls=%async_computation.1 | async-start | bytes 4212736 | tf_op jit(solution)/shard_map/all_gather | solution.py:83
  8.7 299.4 %all-gather.8.cloned.1.call-start = ((), (), s32[]{:S(2)}) async-start(), calls=%async_computation.2 | async-start | bytes 24510464 | tf_op jit(solution)/shard_map/all_gather | solution.py:91
  133.7 19.2 %copy-start.2 = (f32[1408]{0:T(1024)S(1)}, f32[1408]{0:T(1024)}, u32[]{:S(2)}) copy-start(f32[1408]{0:T(1024)} %param.23) | copy-start | bytes 16900
  158.8 0.7 copy-start.3
  158.8 0.7 copy-start.4
  161.2 147.0 %copy-start.10 = (f32[256]{0:T(256)S(1)}, f32[256]{0:T(256)}, u32[]{:S(2)}) copy-start(f32[256]{0:T(256)} %param.27) | copy-start | bytes 3076
  164.8 155.8 %copy-start.1 = (s32[2048]{0:T(1024)S(1)}, s32[2048]{0:T(1024)}, u32[]{:S(2)}) copy-start(s32[2048]{0:T(1024)} %param.17) | copy-start | bytes 24580
Sparse Core Ops, SparseCore 0:
  10.2 90.2 all-gather.3
  102.6 50.2 all-gather.5
  164.9 143.1 all-gather.7
